TPU v7x, 32 devices: a whole 2x2x4 slice. The times are simulated.
32 devices in a mesh: col: 8 (over z, y), row: 4 (over x, core).
Axes of the slice: x: 2, y: 2, z: 4, core: 2. Of those that a mesh axis runs over, the one named last changes fastest.
Arguments:
- panel: float32 [2, 12288, 6144], P(None, 'row', 'col'), may hold values from -0.078125 to 0.078125
- prior: float32 [6144, 64], P('col'), may hold values from -6 to 6
- right_side: float32 [2, 12288, 64], P(None, 'row'), may hold values from -6 to 6
- coupling: float32 [12288, 12288], P('row', 'col'), may hold values from -0.0546875 to 0.0546875
- inverses: float32 [2, 12288, 12288], P(None, 'row', 'col'), as said below
Outputs:
- solved: float32 [2, 12288, 64], P(None, 'row')
Inputs may be any that keep to these rules, and one draw needn't show every extreme that they name: `inverses`: each of the two blocks is zero above its diagonal, and its diagonal lies between 0.5 and 2.
All inputs are finite; a program needn't handle non-finite values.
Results may differ from a plain program's by a relative error of at most 0.00011.
Values sent between devices are 32-bit elements; how exact they have to be, the bound alone decides.
A program may use at most 128 MiB of HBM per device.

v0:
```python
import jax
import jax.numpy as jnp
from jax import lax
from jax.sharding import PartitionSpec as P


def settle(partial_value, base, width):
    tile = base - lax.psum(partial_value, "col")
    whole = lax.all_gather(tile, "row", axis=0, tiled=True)
    segment = lax.dynamic_slice_in_dim(whole, lax.axis_index("col") * width, width, 0)
    return (tile, segment)


def shards(panel, prior, right_side, coupling, inverses):
    highest = lax.Precision.HIGHEST
    width = inverses.shape[2]
    carried = jnp.einsum("bik,kr->bir", panel, prior, precision=highest)
    zeros = jnp.zeros_like(right_side[0])
    first_tile, first_segment = settle(carried[0], right_side[0], width)
    leading_part = jnp.dot(inverses[0], first_segment, precision=highest)
    leading, leading_segment = settle(-leading_part, zeros, width)
    second_part = carried[1] + jnp.dot(coupling, leading_segment, precision=highest)
    second_tile, second_segment = settle(second_part, right_side[1], width)
    trailing_part = jnp.dot(inverses[1], second_segment, precision=highest)
    trailing = lax.psum(trailing_part, "col")
    return jnp.stack([leading, trailing])


def solution(mesh):
    in_specs = (
        P(None, "row", "col"),
        P("col", None),
        P(None, "row", None),
        P("row", "col"),
        P(None, "row", "col"),
    )
    out_specs = P(None, "row", None)
    return jax.shard_map(shards, mesh=mesh, in_specs=in_specs, out_specs=out_specs, check_vma=False)
```

profile of v0, /device:TPU:18, one launch (start us, length us, event | category | flops | bytes accessed | tf_op | source)
XLA Modules:
  0.0 497.4 jit_solution(11359893971080393498)
XLA Ops:
  6.5 0.9 copy-done
  7.5 21.3 %fusion.19 = f32[2,3072,64]{1,2,0:T(8,128)S(1)} fusion(f32[2,3072,768]{2,1,0:T(8,128)} %param.5, f32[768,64]{0,1:T(8,128)S(1)} %copy-done), kind=kOutput, calls=%fused_computation.20 | convolution fusion | flops 3623878656 | bytes 20643840 | tf_op jit(solution)/shard_map/bik,kr->bir/dot_general | solution.py:17
  28.8 0.9 slice_bitcast_fusion.1
  29.7 0.0 all-reduce.5.cloned.1.call-update
  29.7 0.0 all-gather.4.cloned.1.call-start
  29.8 75.2 %all-reduce.5.cloned.1.call-done = f32[3072,64]{0,1:T(8,128)} async-done(((f32[3072,64]{0,1:T(8,128)}), f32[3072,64]{0,1:T(8,128)}) %all-reduce.5.cloned.1.call-update) | async-done | bytes 786448 | tf_op jit(solution)/shard_map/psum | solution.py:8
  105.0 2.1 bitcast_subtract_fusion.1
  107.1 0.2 all-reduce.7.cloned.1.call-start
  107.3 27.7 %all-gather.4.cloned.1.call-done = f32[12288,64]{0,1:T(8,128)} async-done(((f32[3072,64]{0,1:T(8,128)}), f32[12288,64]{0,1:T(8,128)}) %all-gather.4.cloned.1.call-update) | async-done | bytes 3145744 | tf_op jit(solution)/shard_map/all_gather | solution.py:9
  135.1 22.4 %fusion.9 = f32[3072,64]{0,1:T(8,128)} fusion(f32[2,3072,1536]{2,1,0:T(8,128)} %param.9, f32[12288,64]{0,1:T(8,128)} %all-gather.4.cloned.1.call-done, s32[]{:T(128)S(6)} %select_n.2), kind=kOutput, calls=%fused_computation.7 | convolution fusion | flops 3624075264 | bytes 20054020 | tf_op jit(solution)/shard_map/dot_general | solution.py:20
  157.5 0.0 all-gather.6.cloned.1.call-start
  157.5 75.1 %all-reduce.7.cloned.1.call-done = f32[3072,64]{0,1:T(8,128)} async-done(((f32[3072,64]{0,1:T(8,128)}), f32[3072,64]{0,1:T(8,128)}) %all-reduce.7.cloned.1.call-update) | async-done | bytes 786448 | tf_op jit(solution)/shard_map/psum | solution.py:8
  232.7 2.2 fusion.24
  234.9 0.3 all-reduce.9.cloned.1.call-start
  235.1 27.7 %all-gather.6.cloned.1.call-done = f32[12288,64]{0,1:T(8,128)} async-done(((f32[3072,64]{0,1:T(8,128)}), f32[12288,64]{0,1:T(8,128)}) %all-gather.6.cloned.1.call-update) | async-done | bytes 3145744 | tf_op jit(solution)/shard_map/all_gather | solution.py:9
  262.8 22.4 %fusion.15 = f32[3072,64]{0,1:T(8,128)} fusion(f32[3072,1536]{1,0:T(8,128)} %param.8, f32[2,3072,64]{1,2,0:T(8,128)S(1)} %fusion.19, f32[12288,64]{0,1:T(8,128)} %all-gather.6.cloned.1.call-done, s32[]{:T(128)S(6)} %select_n.2), kind=kOutput, calls=%fused_computation.10 | convolution fusion | flops 3624075264 | bytes 20840452 | tf_op jit(solution)/shard_map/dot_general | solution.py:22
  285.3 0.0 all-gather.8.cloned.1.call-start
  285.3 75.0 %all-reduce.9.cloned.1.call-done = f32[3072,64]{0,1:T(8,128)} async-done(((f32[3072,64]{0,1:T(8,128)}), f32[3072,64]{0,1:T(8,128)}) %all-reduce.9.cloned.1.call-update) | async-done | bytes 786448 | tf_op jit(solution)/shard_map/psum | solution.py:8
  360.3 2.3 bitcast_subtract_fusion
  362.7 0.3 all-reduce.11.cloned.1.call-start
  363.0 27.7 %all-gather.8.cloned.1.call-done = f32[12288,64]{0,1:T(8,128)} async-done(((f32[3072,64]{0,1:T(8,128)}), f32[12288,64]{0,1:T(8,128)}) %all-gather.8.cloned.1.call-update) | async-done | bytes 3145744 | tf_op jit(solution)/shard_map/all_gather | solution.py:9
  390.6 22.4 %fusion.12 = f32[1,3072,64]{1,2,0:T(8,128)} fusion(f32[2,3072,1536]{2,1,0:T(8,128)} %param.9, f32[12288,64]{0,1:T(8,128)} %all-gather.8.cloned.1.call-done, s32[]{:T(128)S(6)} %select_n.2), kind=kOutput, calls=%fused_computation.8 | convolution fusion | flops 3623878656 | bytes 20054020 | tf_op jit(solution)/shard_map/dot_general | solution.py:24
  413.1 75.1 %all-reduce.11.cloned.1.call-done = f32[1,3072,64]{1,2,0:T(8,128)} async-done(((f32[1,3072,64]{1,2,0:T(8,128)}), f32[1,3072,64]{1,2,0:T(8,128)}) %all-reduce.11.cloned.1.call-update) | async-done | bytes 786448 | tf_op jit(solution)/shard_map/psum | solution.py:25
  488.2 2.4 pad_maximum_fusion
  (12 shorter events, 0.1 us)
Async XLA Ops:
  6.5 0.9 copy-start
  6.5 98.4 %copy-start.2 = (f32[2,3072,64]{1,2,0:T(8,128)S(1)}, f32[2,3072,64]{1,2,0:T(8,128)}, u32[]{:S(2)}) copy-start(f32[2,3072,64]{1,2,0:T(8,128)} %param.7) | copy-start | bytes 4718596
  6.5 98.4 %all-reduce.5.cloned.1.call-start = ((), (), s32[]{:S(2)}) async-start(), calls=%async_computation | async-start | bytes 1572864 | tf_op jit(solution)/shard_map/psum | solution.py:8
  29.7 105.3 %all-gather.4.cloned.1.call-start = ((), (), s32[]{:S(2)}) async-start(), calls=%async_computation.1 | async-start | bytes 3932160 | tf_op jit(solution)/shard_map/all_gather | solution.py:9
  107.1 125.6 %all-reduce.7.cloned.1.call-start = ((), (), s32[]{:S(2)}) async-start(), calls=%async_computation.2 | async-start | bytes 1572864 | tf_op jit(solution)/shard_map/psum | solution.py:8
  157.5 105.3 %all-gather.6.cloned.1.call-start = ((), (), s32[]{:S(2)}) async-start(), calls=%async_computation.3 | async-start | bytes 3932160 | tf_op jit(solution)/shard_map/all_gather | solution.py:9
  234.9 125.4 %all-reduce.9.cloned.1.call-start = ((), (), s32[]{:S(2)}) async-start(), calls=%async_computation.4 | async-start | bytes 1572864 | tf_op jit(solution)/shard_map/psum | solution.py:8
  285.3 105.3 %all-gather.8.cloned.1.call-start = ((), (), s32[]{:S(2)}) async-start(), calls=%async_computation.5 | async-start | bytes 3932160 | tf_op jit(solution)/shard_map/all_gather | solution.py:9
  362.7 125.5 %all-reduce.11.cloned.1.call-start = ((), (), s32[]{:S(2)}) async-start(), calls=%async_computation.6 | async-start | bytes 1572864 | tf_op jit(solution)/shard_map/psum | solution.py:25
  390.6 100.0 %copy-start.1 = (f32[768,64]{0,1:T(8,128)S(1)}, f32[768,64]{0,1:T(8,128)}, u32[]{:S(2)}) copy-start(f32[768,64]{0,1:T(8,128)} %param.6) | copy-start | bytes 589828
Sparse Core Ops, SparseCore 0:
  29.9 75.0 all-reduce.4
  107.2 27.7 all-gather.3
  157.6 75.0 all-reduce.6
  235.0 27.7 all-gather.5
  285.4 74.8 all-reduce.8
  362.8 27.7 all-gather.7
  413.2 74.9 all-reduce.10
where the time goes:
time: 500 us; the launch traced here: 497 us
  waiting for transfers between devices  384 us (77%)
  matrix products  88.6 us (18%)
  between operations  13.5 us (3%)
  other arithmetic  8.98 us (2%)
    psum x3, waiting for transfers between devices, settle(): tile = base - lax.psum(partial_value, 'col')  225 us
    all_gather x3, waiting for transfers between devices, settle(): whole = lax.all_gather(tile, 'row', axis=0, tiled=True)  83.1 us
    psum x1, waiting for transfers between devices, shards(): trailing = lax.psum(trailing_part, 'col')  75.1 us
    dot_general x1, matrix products, shards(): trailing_part = jnp.dot(inverses[1], second_segment, precision=highest)  22.4 us
    dot_general x1, matrix products, shards(): leading_part = jnp.dot(inverses[0], first_segment, precision=highest)  22.4 us
    dot_general x1, matrix products, shards(): jnp.dot(coupling, leading_segment, precision=highest)  22.4 us
    dot_general x1, matrix products, shards(): carried = jnp.einsum('bik,kr->bir', panel, prior, precision=highest)  21.3 us
  transfers between devices with their start and end apart: 7, of which 7 were waited for; matrix products, arithmetic and copies ran while one was open for 0% of the time, Pallas kernels for 0%

commit v1 on v0

v1 whole, which is shorter than its diff:
```python
import functools
import jax
import jax.numpy as jnp
from jax import lax
from jax.experimental import pallas as pl
from jax.experimental.pallas import tpu as pltpu
from jax.sharding import PartitionSpec as P

F32, BF16 = jnp.float32, jnp.bfloat16


def kernel(q, nr, panel, prior, rs, coup, inv, out, part, part1, ra, rb, tv, xv, wv, w0, pbuf, buf0, buf1, rsv,
           psem, sem0, sem1, rsem, a_s, a_r, b_s, b_r, c1_s, x_r, c2_s, d_s, d_r, dy_s, dy_r):
    zn = nr
    nx = nr // 2
    hp = part.shape[2]
    pr = 2 * hp
    r = prior.shape[1]
    nb = q * zn
    col = lax.axis_index("col")
    i = lax.axis_index("row")
    z, y = lax.div(col, q), lax.rem(col, q)
    low = lax.broadcasted_iota(jnp.int32, (hp, 2 * r), 1) < r
    below = z <= i
    hub = z == i
    relay = jnp.logical_and(lax.rem(i, 2) == lax.rem(z, 2), lax.div(i, 2) != lax.div(z, 2))
    sibling = i + 1 - 2 * lax.rem(i, 2)

    def dev(zz, yy, ii):
        return {"col": zz * q + yy, "row": ii}

    def zfwd(k):
        return lax.rem(z + 1 + k, zn)

    def zback(k):
        return lax.rem(z + zn - 1 - k, zn)

    def yfwd(m):
        return lax.rem(y + 1 + m, q)

    def yback(m):
        return lax.rem(y + q - 1 - m, q)

    def remote(src, dst, ss, rr, to):
        return pltpu.make_async_remote_copy(
            src_ref=src, dst_ref=dst, send_sem=ss, recv_sem=rr, device_id=to, device_id_type=pl.DeviceIdType.MESH)

    def rows_of(m, k):
        return pl.ds(pl.multiple_of((yfwd(m) * zn + zfwd(k)) * pr, pr), pr)

    def load(src, dst, sem, m, k):
        rows = rows_of(m, k)
        return pltpu.make_async_copy(src.at[rows, :], dst.at[rows, :], sem.at[m * zn + k])

    def load_all(src, dst, sem):
        for m in range(q):
            pl.loop(0, zn)(lambda k, m=m: load(src, dst, sem, m, k).start())

    load_all(panel.at[0], pbuf, psem)
    mine = pl.ds(pl.multiple_of((y * zn + z) * pr, pr), pr)
    rs_copies = [pltpu.make_async_copy(rs.at[b, mine, :], rsv.at[b], rsem.at[b]) for b in range(2)]
    for c in rs_copies:
        c.start()
    pl.when(below)(lambda: load_all(inv.at[0], buf0, sem0))

    barrier = pltpu.get_barrier_semaphore()
    for k in range(zn - 1):
        pl.semaphore_signal(barrier, inc=1, device_id=dev(zfwd(k), y, i), device_id_type=pl.DeviceIdType.MESH)
    for m in range(q - 1):
        pl.semaphore_signal(barrier, inc=1, device_id=dev(z, yfwd(m), i), device_id_type=pl.DeviceIdType.MESH)
    for n in range(nr - 1):
        pl.semaphore_signal(barrier, inc=1, device_id=dev(z, y, lax.rem(i + 1 + n, nr)), device_id_type=pl.DeviceIdType.MESH)

    def split(d):
        n = d.shape[0]
        lo = lax.broadcasted_iota(jnp.int32, (n, 2 * r), 1) < r
        return jnp.where(lo, d, d - d.astype(BF16).astype(F32)).astype(BF16)

    v = prior[...]
    w0[...] = split(jnp.concatenate([v, v], axis=1))
    for c in rs_copies:
        c.wait()

    def base(b):
        return jnp.concatenate([rsv[b, :hp, :], rsv[b, hp:, :]], axis=1)

    pl.semaphore_wait(barrier, zn - 1 + q - 1 + nr - 1)

    def product(buf, w, m, k):
        a = buf[rows_of(m, k), :]
        a1 = a.astype(BF16)
        a2 = (a - a1.astype(F32)).astype(BF16)
        p = jnp.dot(jnp.concatenate([a1, a2], axis=0), w[...], preferred_element_type=F32)
        s = p[:pr] + p[pr:]
        s = s + pltpu.roll(s, r, 1)
        return jnp.where(low, s[:hp], s[hp:])

    def a_copy(ph, m, k):
        return remote(part.at[yfwd(m), zfwd(k)], ra.at[ph, m, k], a_s.at[ph, m, k], a_r.at[ph, m, k], dev(z, yfwd(m), i))

    def b_copy(ph, k):
        return remote(part.at[y, zfwd(k)], rb.at[ph, k], b_s.at[ph, k], b_r.at[ph, k], dev(zfwd(k), y, i))

    def guard(tri, cond, f):
        if tri:
            pl.when(cond)(f)
        else:
            f()

    def reduce(ph, src, buf, sem, w, tri, rhs, add=False, after=None, middle=None):
        def compute():
            for m in range(q):
                @pl.loop(0, zn)
                def _(k):
                    load(src, buf, sem, m, k).wait()
                    val = product(buf, w, m, k)
                    if add:
                        val = val + part1[yfwd(m), zfwd(k)]
                    part[yfwd(m), zfwd(k)] = val
                    if m < q - 1:
                        a_copy(ph, m, k).start()
                    if after is not None:
                        load(after, buf, sem, m, k).start()

        guard(tri, below, compute)
        if middle is not None:
            middle()

        def collect():
            def one(k):
                val = part[y, zfwd(k)]
                for m in range(q - 1):
                    a_copy(ph, m, k).wait_recv()
                    val = val + ra[ph, m, k]
                part[y, zfwd(k)] = val

            @pl.loop(0, zn - 1)
            def _(k):
                one(k)
                b_copy(ph, k).start()

            one(zn - 1)

        guard(tri, below, collect)
        if tri:
            @pl.when(jnp.logical_not(below))
            def _():
                part[y, z] = jnp.zeros((hp, 2 * r), F32)
        for k in range(zn - 1):
            def take(k=k):
                b_copy(ph, k).wait_recv()
                part[y, z] = part[y, z] + rb[ph, k]

            guard(tri, zback(k) <= i, take)
        tv[ph] = part[y, z] if rhs is None else base(rhs) - part[y, z]

    def drain(ph, tri):
        def waits():
            for m in range(q - 1):
                pl.loop(0, zn)(lambda k, m=m: a_copy(ph, m, k).wait_send())
            pl.loop(0, zn - 1)(lambda k: b_copy(ph, k).wait_send())

        guard(tri, below, waits)

    def spread(ph):
        up = remote(tv.at[ph], xv.at[ph, z], c1_s.at[ph], x_r.at[ph, z], dev(i, y, i))

        def fwd(s, n):
            to = sibling if n == 0 else lax.rem(i + 2 * n, nr)
            return remote(xv.at[ph, s], xv.at[ph, s], c2_s.at[ph, s, n], x_r.at[ph, s], dev(z, y, to))

        @pl.when(hub)
        def _():
            xv[ph, z] = tv[ph]

        pl.when(jnp.logical_not(hub))(lambda: up.start())

        @pl.loop(0, zn)
        def _(k):
            s = lax.rem(z + k, zn)
            pl.when(jnp.logical_not(jnp.logical_and(hub, s == z)))(lambda: fwd(s, 0).wait_recv())

            @pl.when(hub)
            def _():
                for n in range(1, nx):
                    fwd(s, n).start()
                fwd(s, 0).start()

            pl.when(relay)(lambda: fwd(s, 0).start())
            u = xv[ph, s]
            ur = pltpu.roll(u, r, 1)
            at = pl.multiple_of(s * pr, pr)
            wv[pl.ds(at, pr), :] = jnp.concatenate(
                [split(jnp.where(low, u, ur)), split(jnp.where(low, ur, u))], axis=0)

        def finish():
            pl.when(jnp.logical_not(hub))(lambda: up.wait_send())

            @pl.when(hub)
            def _():
                @pl.loop(0, zn)
                def _(s):
                    for n in range(nx):
                        fwd(s, n).wait_send()

            @pl.when(relay)
            def _():
                pl.loop(0, zn)(lambda s: fwd(s, 0).wait_send())

        return finish

    def dz_copy(b, ph, k):
        return remote(tv.at[ph], out.at[b, y, z], d_s.at[b, k], d_r.at[b, k], dev(zfwd(k), y, i))

    def dy_copy(b, m, slot, s):
        return remote(out.at[b, y, s], out.at[b, y, s], dy_s.at[b, m, slot], dy_r.at[b, m, slot], dev(z, yfwd(m), i))

    def publish_z(b, ph):
        out[b, y, z] = tv[ph]
        for k in range(zn - 1):
            dz_copy(b, ph, k).start()

    def publish_y(b, ph):
        for m in range(q - 1):
            dy_copy(b, m, 0, z).start()
        for k in range(zn - 1):
            remote(tv.at[ph], out.at[b, y, zback(k)], d_s.at[b, k], d_r.at[b, k], dev(zfwd(k), y, i)).wait_recv()
            for m in range(q - 1):
                dy_copy(b, m, k + 1, zback(k)).start()

    def publish_end(b, ph):
        for slot in range(zn):
            s = z if slot == 0 else zback(slot - 1)
            for m in range(q - 1):
                there = out.at[b, yback(m), s]
                remote(there, there, dy_s.at[b, m, slot], dy_r.at[b, m, slot], dev(z, yfwd(m), i)).wait_recv()
                dy_copy(b, m, slot, s).wait_send()
        for k in range(zn - 1):
            dz_copy(b, ph, k).wait_send()

    def second_carried():
        for m in range(q):
            @pl.loop(0, zn)
            def _(k):
                load(panel.at[1], pbuf, psem, m, k).wait()
                part1[yfwd(m), zfwd(k)] = product(pbuf, w0, m, k)

    reduce(0, panel.at[0], pbuf, psem, w0, False, 0, after=panel.at[1], middle=second_carried)
    load_all(coup, buf1, sem1)
    end0 = spread(0)
    drain(0, False)
    reduce(1, inv.at[0], buf0, sem0, wv, True, None, after=inv.at[1])
    end1 = spread(1)
    drain(1, True)
    publish_z(0, 1)
    reduce(2, coup, buf1, sem1, wv, False, 1, add=True)
    end2 = spread(2)
    drain(2, False)
    publish_y(0, 1)
    reduce(3, inv.at[1], buf0, sem0, wv, True, None)
    publish_z(1, 3)
    publish_y(1, 3)
    drain(3, True)
    end0()
    end1()
    end2()
    publish_end(0, 1)
    publish_end(1, 3)


def shards(nc, nr, panel, prior, right_side, coupling, inverses):
    q = nc // nr
    rows, width = coupling.shape
    r = prior.shape[1]
    hp = rows // (q * nr * 2)
    lanes = 2 * r
    dma = pltpu.SemaphoreType.DMA
    hbm = pl.BlockSpec(memory_space=pl.ANY)
    vmem = pl.BlockSpec(memory_space=pltpu.VMEM)
    packed = pl.pallas_call(
        functools.partial(kernel, q, nr),
        out_shape=jax.ShapeDtypeStruct((2, q, nr, hp, lanes), F32),
        in_specs=[hbm, vmem, hbm, hbm, hbm],
        out_specs=vmem,
        scratch_shapes=[
            pltpu.VMEM((q, nr, hp, lanes), F32),
            pltpu.VMEM((q, nr, hp, lanes), F32),
            pltpu.VMEM((4, q - 1, nr, hp, lanes), F32),
            pltpu.VMEM((4, nr - 1, hp, lanes), F32),
            pltpu.VMEM((4, hp, lanes), F32),
            pltpu.VMEM((3, nr, hp, lanes), F32),
            pltpu.VMEM((width, lanes), BF16),
            pltpu.VMEM((prior.shape[0], lanes), BF16),
            pltpu.VMEM(panel.shape[1:], F32),
            pltpu.VMEM((rows, width), F32),
            pltpu.VMEM((rows, width), F32),
            pltpu.VMEM((2, 2 * hp, r), F32),
            dma((nc,)), dma((nc,)), dma((nc,)), dma((2,)),
            dma((4, q - 1, nr)), dma((4, q - 1, nr)),
            dma((4, nr - 1)), dma((4, nr - 1)),
            dma((3,)), dma((3, nr)), dma((3, nr, nr // 2)),
            dma((2, nr - 1)), dma((2, nr - 1)),
            dma((2, q - 1, nr)), dma((2, q - 1, nr)),
        ],
        compiler_params=pltpu.CompilerParams(collective_id=0, has_side_effects=True, vmem_limit_bytes=67043328),
    )(panel, prior, right_side, coupling, inverses)
    whole = packed.reshape(2, nc, hp, 2, r).transpose(0, 1, 3, 2, 4)
    return whole.reshape(2, rows, r)


def solution(mesh):
    in_specs = (
        P(None, "row", "col"),
        P("col", None),
        P(None, "row", None),
        P("row", "col"),
        P(None, "row", "col"),
    )
    out_specs = P(None, "row", None)
    body = functools.partial(shards, mesh.shape["col"], mesh.shape["row"])
    return jax.shard_map(body, mesh=mesh, in_specs=in_specs, out_specs=out_specs, check_vma=False)
```

time: 500 us -> 143 us (0.29)
  waiting for transfers between devices: 384 us -> 0 us
  Pallas kernels: 0 us -> 126 us
  matrix products: 88.6 us -> 0 us
  between operations: 13.5 us -> 0.02 us
  local copies, waits for them, and re-layouts: 1.86 us -> 13.9 us
  other arithmetic: 8.98 us -> 0 us
    psum x4 -> x0, waiting for transfers between devices: 300 us -> none  [the longest x3 225 us: settle(): tile = base - lax.psum(partial_value, 'col')]
    pallas_call x0 -> x1, Pallas kernels: none -> 126 us  [shards(): pl.pallas_call(functools.partial(kernel, q, nr), out_shape=jax.ShapeDtype...]
    dot_general x4 -> x0, matrix products: 88.6 us -> none  [the longest x1 22.4 us: shards(): trailing_part = jnp.dot(inverses[1], second_segment, precision=highest)]
    all_gather x3 -> x0, waiting for transfers between devices: 83.1 us -> none  [settle(): whole = lax.all_gather(tile, 'row', axis=0, tiled=True)]
  transfers between devices with their start and end apart: 7 -> 0, of which waited for: 7 -> 0; matrix products, arithmetic and copies ran while one was open for 0% -> 0% of each run, Pallas kernels for 0% -> 0%
where the time goes in v1:
time: 143 us; the launch traced here: 140 us
  Pallas kernels  126 us (88%)
  local copies, waits for them, and re-layouts  13.9 us (10%)
    pallas_call x1, Pallas kernels, shards(): pl.pallas_call(functools.partial(kernel, q, nr), out_shape=jax.ShapeDtype...  126 us
    unnamed x2, local copies, waits for them, and re-layouts  5.12 us
    reshape x1, local copies, waits for them, and re-layouts, shards(): return whole.reshape(2, rows, r)  3.98 us
    transpose x1, local copies, waits for them, and re-layouts, shards(): whole = packed.reshape(2, nc, hp, 2, r).transpose(0, 1, 3, 2, 4)  2.97 us

profile of v1, /device:TPU:18, one launch (start us, length us, event | category | flops | bytes accessed | tf_op | source)
XLA Modules:
  0.0 140.3 jit_solution(2082377334986046036)
XLA Ops:
  0.0 1.8 %copy.12.prior = f32[768,64]{1,0:T(8,128)} copy(f32[768,64]{0,1:T(8,128)} %param.6) | data formatting | bytes 393216 | tf_op args[1]
  1.8 3.3 %copy.13.rs = f32[2,3072,64]{2,1,0:T(8,128)} copy(f32[2,3072,64]{1,2,0:T(8,128)} %param.7) | data formatting | bytes 3145728 | tf_op args[2]
  5.1 126.4 %shard_map.55 = f32[2,2,4,192,128]{4,3,2,1,0:T(8,128)} custom-call(f32[2,3072,768]{2,1,0:T(8,128)} %panel.1, f32[768,64]{1,0:T(8,128)} %copy.12.prior, f32[2,3072,64]{2,1,0:T(8,128)} %copy.13.rs, f32[3072,1536]{1,0:T(8,128)} %coup.1, f32[2,3072,1536]{2,1,0:T(8,128)} %inv.1), custom_call_target="tpu_custom_call" | custom-call | tf_op jit(solution)/shard_map/pallas_call | solution.py:280
  131.5 1.8 %copy.14 = f32[2,2,4,192,128]{3,4,2,1,0:T(8,128)S(1)} copy(f32[2,2,4,192,128]{4,3,2,1,0:T(8,128)} %shard_map.55) | data formatting | bytes 3145728 | tf_op jit(solution)/shard_map/pallas_call | solution.py:280
  133.3 3.0 %copy.15 = f32[2,8,2,192,64]{3,2,1,4,0:T(2,128)} copy(f32[2,8,2,192,64]{3,4,2,1,0:T(8,128)S(1)} %bitcast.5) | data formatting | bytes 3145728 | tf_op jit(solution)/shard_map/transpose | solution.py:307
  136.3 4.0 %reshape.7 = f32[2,3072,64]{1,2,0:T(8,128)} reshape(f32[2,8,2,192,64]{3,2,1,4,0:T(2,128)} %copy.15) | data formatting | bytes 3145728 | tf_op jit(solution)/shard_map/reshape | solution.py:308

commit v2 on v1

--- a/solution.py
+++ b/solution.py
@@ -13,17 +13,14 @@
            psem, sem0, sem1, rsem, a_s, a_r, b_s, b_r, c1_s, x_r, c2_s, d_s, d_r, dy_s, dy_r):
     zn = nr
     nx = nr // 2
-    hp = part.shape[2]
-    pr = 2 * hp
-    r = prior.shape[1]
-    nb = q * zn
+    r, pr = part.shape[2:]
     col = lax.axis_index("col")
     i = lax.axis_index("row")
     z, y = lax.div(col, q), lax.rem(col, q)
-    low = lax.broadcasted_iota(jnp.int32, (hp, 2 * r), 1) < r
     below = z <= i
     hub = z == i
-    relay = jnp.logical_and(lax.rem(i, 2) == lax.rem(z, 2), lax.div(i, 2) != lax.div(z, 2))
+    direct = lax.rem(i, 2) == lax.rem(z, 2)
+    far = jnp.logical_and(direct, jnp.logical_not(hub))
     sibling = i + 1 - 2 * lax.rem(i, 2)
 
     def dev(zz, yy, ii):
@@ -57,8 +54,13 @@
             pl.loop(0, zn)(lambda k, m=m: load(src, dst, sem, m, k).start())
 
     load_all(panel.at[0], pbuf, psem)
-    mine = pl.ds(pl.multiple_of((y * zn + z) * pr, pr), pr)
-    rs_copies = [pltpu.make_async_copy(rs.at[b, mine, :], rsv.at[b], rsem.at[b]) for b in range(2)]
+
+    def piece(ref, b, yy, zz):
+        if len(ref.shape) == 4:
+            return ref.at[b, yy * zn + zz]
+        return ref.at[b, :, pl.ds(pl.multiple_of((yy * zn + zz) * pr, pr), pr)]
+
+    rs_copies = [pltpu.make_async_copy(piece(rs, b, y, z), rsv.at[b], rsem.at[b]) for b in range(2)]
     for c in rs_copies:
         c.start()
     pl.when(below)(lambda: load_all(inv.at[0], buf0, sem0))
@@ -71,29 +73,27 @@
     for n in range(nr - 1):
         pl.semaphore_signal(barrier, inc=1, device_id=dev(z, y, lax.rem(i + 1 + n, nr)), device_id_type=pl.DeviceIdType.MESH)
 
-    def split(d):
-        n = d.shape[0]
-        lo = lax.broadcasted_iota(jnp.int32, (n, 2 * r), 1) < r
-        return jnp.where(lo, d, d - d.astype(BF16).astype(F32)).astype(BF16)
-
-    v = prior[...]
-    w0[...] = split(jnp.concatenate([v, v], axis=1))
+    @pl.when(far)
+    def _():
+        for k in range(zn):
+            pl.semaphore_signal(barrier, inc=1, device_id=dev(k, y, z), device_id_type=pl.DeviceIdType.MESH)
+
+    def split(x):
+        high = x.astype(BF16).astype(F32)
+        return jnp.concatenate([high, x - high], axis=0).T.astype(BF16)
+
+    w0[...] = split(prior[...])
     for c in rs_copies:
         c.wait()
-
-    def base(b):
-        return jnp.concatenate([rsv[b, :hp, :], rsv[b, hp:, :]], axis=1)
-
-    pl.semaphore_wait(barrier, zn - 1 + q - 1 + nr - 1)
+    pl.semaphore_wait(barrier, zn - 1 + q - 1 + nr - 1 + nx - 1)
 
     def product(buf, w, m, k):
         a = buf[rows_of(m, k), :]
         a1 = a.astype(BF16)
         a2 = (a - a1.astype(F32)).astype(BF16)
         p = jnp.dot(jnp.concatenate([a1, a2], axis=0), w[...], preferred_element_type=F32)
-        s = p[:pr] + p[pr:]
-        s = s + pltpu.roll(s, r, 1)
-        return jnp.where(low, s[:hp], s[hp:])
+        s = (p[:pr] + p[pr:]).T
+        return s[:r] + s[r:]
 
     def a_copy(ph, m, k):
         return remote(part.at[yfwd(m), zfwd(k)], ra.at[ph, m, k], a_s.at[ph, m, k], a_r.at[ph, m, k], dev(z, yfwd(m), i))
@@ -145,14 +145,14 @@
         if tri:
             @pl.when(jnp.logical_not(below))
             def _():
-                part[y, z] = jnp.zeros((hp, 2 * r), F32)
+                part[y, z] = jnp.zeros((r, pr), F32)
         for k in range(zn - 1):
             def take(k=k):
                 b_copy(ph, k).wait_recv()
                 part[y, z] = part[y, z] + rb[ph, k]
 
             guard(tri, zback(k) <= i, take)
-        tv[ph] = part[y, z] if rhs is None else base(rhs) - part[y, z]
+        tv[ph] = part[y, z] if rhs is None else rsv[rhs] - part[y, z]
 
     def drain(ph, tri):
         def waits():
@@ -163,60 +163,43 @@
         guard(tri, below, waits)
 
     def spread(ph):
-        up = remote(tv.at[ph], xv.at[ph, z], c1_s.at[ph], x_r.at[ph, z], dev(i, y, i))
-
-        def fwd(s, n):
-            to = sibling if n == 0 else lax.rem(i + 2 * n, nr)
-            return remote(xv.at[ph, s], xv.at[ph, s], c2_s.at[ph, s, n], x_r.at[ph, s], dev(z, y, to))
+        def up(n):
+            return remote(tv.at[ph], xv.at[ph, z], c1_s.at[ph, n], x_r.at[ph, z], dev(i, y, lax.rem(i + 2 * n, nr)))
+
+        def fwd(s):
+            return remote(xv.at[ph, s], xv.at[ph, s], c2_s.at[ph, s], x_r.at[ph, s], dev(z, y, sibling))
 
         @pl.when(hub)
         def _():
             xv[ph, z] = tv[ph]
 
-        pl.when(jnp.logical_not(hub))(lambda: up.start())
+        for n in range(1, nx):
+            up(n).start()
+        pl.when(jnp.logical_not(hub))(lambda: up(0).start())
 
         @pl.loop(0, zn)
         def _(k):
             s = lax.rem(z + k, zn)
-            pl.when(jnp.logical_not(jnp.logical_and(hub, s == z)))(lambda: fwd(s, 0).wait_recv())
-
-            @pl.when(hub)
-            def _():
-                for n in range(1, nx):
-                    fwd(s, n).start()
-                fwd(s, 0).start()
-
-            pl.when(relay)(lambda: fwd(s, 0).start())
-            u = xv[ph, s]
-            ur = pltpu.roll(u, r, 1)
-            at = pl.multiple_of(s * pr, pr)
-            wv[pl.ds(at, pr), :] = jnp.concatenate(
-                [split(jnp.where(low, u, ur)), split(jnp.where(low, ur, u))], axis=0)
+            pl.when(jnp.logical_not(jnp.logical_and(hub, s == z)))(lambda: fwd(s).wait_recv())
+            pl.when(direct)(lambda: fwd(s).start())
+            wv[pl.ds(pl.multiple_of(s * pr, pr), pr), :] = split(xv[ph, s])
 
         def finish():
-            pl.when(jnp.logical_not(hub))(lambda: up.wait_send())
-
-            @pl.when(hub)
-            def _():
-                @pl.loop(0, zn)
-                def _(s):
-                    for n in range(nx):
-                        fwd(s, n).wait_send()
-
-            @pl.when(relay)
-            def _():
-                pl.loop(0, zn)(lambda s: fwd(s, 0).wait_send())
+            for n in range(1, nx):
+                up(n).wait_send()
+            pl.when(jnp.logical_not(hub))(lambda: up(0).wait_send())
+            pl.when(direct)(lambda: pl.loop(0, zn)(lambda s: fwd(s).wait_send()))
 
         return finish
 
     def dz_copy(b, ph, k):
-        return remote(tv.at[ph], out.at[b, y, z], d_s.at[b, k], d_r.at[b, k], dev(zfwd(k), y, i))
+        return remote(tv.at[ph], piece(out, b, y, z), d_s.at[b, k], d_r.at[b, k], dev(zfwd(k), y, i))
 
     def dy_copy(b, m, slot, s):
-        return remote(out.at[b, y, s], out.at[b, y, s], dy_s.at[b, m, slot], dy_r.at[b, m, slot], dev(z, yfwd(m), i))
+        return remote(piece(out, b, y, s), piece(out, b, y, s), dy_s.at[b, m, slot], dy_r.at[b, m, slot], dev(z, yfwd(m), i))
 
     def publish_z(b, ph):
-        out[b, y, z] = tv[ph]
+        piece(out, b, y, z)[...] = tv[ph]
         for k in range(zn - 1):
             dz_copy(b, ph, k).start()
 
@@ -224,7 +207,7 @@
         for m in range(q - 1):
             dy_copy(b, m, 0, z).start()
         for k in range(zn - 1):
-            remote(tv.at[ph], out.at[b, y, zback(k)], d_s.at[b, k], d_r.at[b, k], dev(zfwd(k), y, i)).wait_recv()
+            remote(tv.at[ph], piece(out, b, y, zback(k)), d_s.at[b, k], d_r.at[b, k], dev(zfwd(k), y, i)).wait_recv()
             for m in range(q - 1):
                 dy_copy(b, m, k + 1, zback(k)).start()
 
@@ -232,7 +215,7 @@
         for slot in range(zn):
             s = z if slot == 0 else zback(slot - 1)
             for m in range(q - 1):
-                there = out.at[b, yback(m), s]
+                there = piece(out, b, yback(m), s)
                 remote(there, there, dy_s.at[b, m, slot], dy_r.at[b, m, slot], dev(z, yfwd(m), i)).wait_recv()
                 dy_copy(b, m, slot, s).wait_send()
         for k in range(zn - 1):
@@ -272,40 +255,45 @@
     q = nc // nr
     rows, width = coupling.shape
     r = prior.shape[1]
-    hp = rows // (q * nr * 2)
+    pr = rows // nc
+    dense = pr % 128 == 0
     lanes = 2 * r
     dma = pltpu.SemaphoreType.DMA
     hbm = pl.BlockSpec(memory_space=pl.ANY)
     vmem = pl.BlockSpec(memory_space=pltpu.VMEM)
-    packed = pl.pallas_call(
+    side = right_side.transpose(0, 2, 1)
+    if not dense:
+        side = side.reshape(2, r, nc, pr).transpose(0, 2, 1, 3)
+    solved = pl.pallas_call(
         functools.partial(kernel, q, nr),
-        out_shape=jax.ShapeDtypeStruct((2, q, nr, hp, lanes), F32),
+        out_shape=jax.ShapeDtypeStruct(side.shape, F32),
         in_specs=[hbm, vmem, hbm, hbm, hbm],
         out_specs=vmem,
         scratch_shapes=[
-            pltpu.VMEM((q, nr, hp, lanes), F32),
-            pltpu.VMEM((q, nr, hp, lanes), F32),
-            pltpu.VMEM((4, q - 1, nr, hp, lanes), F32),
-            pltpu.VMEM((4, nr - 1, hp, lanes), F32),
-            pltpu.VMEM((4, hp, lanes), F32),
-            pltpu.VMEM((3, nr, hp, lanes), F32),
+            pltpu.VMEM((q, nr, r, pr), F32),
+            pltpu.VMEM((q, nr, r, pr), F32),
+            pltpu.VMEM((4, q - 1, nr, r, pr), F32),
+            pltpu.VMEM((4, nr - 1, r, pr), F32),
+            pltpu.VMEM((4, r, pr), F32),
+            pltpu.VMEM((3, nr, r, pr), F32),
             pltpu.VMEM((width, lanes), BF16),
             pltpu.VMEM((prior.shape[0], lanes), BF16),
             pltpu.VMEM(panel.shape[1:], F32),
             pltpu.VMEM((rows, width), F32),
             pltpu.VMEM((rows, width), F32),
-            pltpu.VMEM((2, 2 * hp, r), F32),
+            pltpu.VMEM((2, r, pr), F32),
             dma((nc,)), dma((nc,)), dma((nc,)), dma((2,)),
             dma((4, q - 1, nr)), dma((4, q - 1, nr)),
             dma((4, nr - 1)), dma((4, nr - 1)),
-            dma((3,)), dma((3, nr)), dma((3, nr, nr // 2)),
+            dma((3, nr // 2)), dma((3, nr)), dma((3, nr)),
             dma((2, nr - 1)), dma((2, nr - 1)),
             dma((2, q - 1, nr)), dma((2, q - 1, nr)),
         ],
         compiler_params=pltpu.CompilerParams(collective_id=0, has_side_effects=True, vmem_limit_bytes=67043328),
-    )(panel, prior, right_side, coupling, inverses)
-    whole = packed.reshape(2, nc, hp, 2, r).transpose(0, 1, 3, 2, 4)
-    return whole.reshape(2, rows, r)
+    )(panel, prior.T, side, coupling, inverses)
+    if not dense:
+        solved = solved.transpose(0, 2, 1, 3).reshape(2, r, rows)
+    return solved.transpose(0, 2, 1)
 
 
 def solution(mesh):

time: 143 us -> 131 us (0.916); the launches traced: 140 us -> 131 us
  local copies, waits for them, and re-layouts: 13.9 us -> 2.7 us
  Pallas kernels: 126 us -> 128 us
    reshape x1 -> x0, local copies, waits for them, and re-layouts: 3.98 us -> none  [shards(): return whole.reshape(2, rows, r)]
    transpose x1 -> x0, local copies, waits for them, and re-layouts: 2.97 us -> none  [shards(): whole = packed.reshape(2, nc, hp, 2, r).transpose(0, 1, 3, 2, 4)]
    unnamed x2 -> x1, local copies, waits for them, and re-layouts: 5.12 us -> 2.7 us
    pallas_call x1 -> x0, local copies, waits for them, and re-layouts: 1.83 us -> none  [shards(): pl.pallas_call(functools.partial(kernel, q, nr), out_shape=jax.ShapeDtype...]
    pallas_call x1, Pallas kernels: 126 us -> 128 us  [shards(): pl.pallas_call(functools.partial(kernel, q, nr), out_shape=jax.ShapeDtype...]
where the time goes in v2:
time: 131 us
  Pallas kernels  128 us (98%)
  local copies, waits for them, and re-layouts  2.7 us (2%)
    pallas_call x1, Pallas kernels, shards(): pl.pallas_call(functools.partial(kernel, q, nr), out_shape=jax.ShapeDtype...  128 us
    unnamed x1, local copies, waits for them, and re-layouts  2.7 us

profile of v2, /device:TPU:18, one launch (start us, length us, event | category | flops | bytes accessed | tf_op | source)
XLA Modules:
  0.0 130.9 jit_solution(13575530981380390332)
XLA Ops:
  0.0 128.2 %shard_map.55 = f32[2,64,3072]{2,1,0:T(8,128)} custom-call(f32[2,3072,768]{2,1,0:T(8,128)} %panel.1, f32[64,768]{1,0:T(8,128)} %bitcast.5, f32[2,64,3072]{2,1,0:T(8,128)} %bitcast.4, f32[3072,1536]{1,0:T(8,128)} %coup.1, f32[2,3072,1536]{2,1,0:T(8,128)} %inv.1), custom_call_target="tpu_custom_call" | custom-call | tf_op jit(solution)/shard_map/pallas_call | solution.py:267
  128.2 2.7 %copy.7 = f32[2,3072,64]{1,2,0:T(8,128)} copy(f32[2,3072,64]{1,2,0:T(8,128)} %bitcast.3) | data formatting | bytes 3145728

commit v3 on v2

--- a/solution.py
+++ b/solution.py
@@ -7,6 +7,7 @@
 from jax.sharding import PartitionSpec as P
 
 F32, BF16 = jnp.float32, jnp.bfloat16
+SUBS = 2
 
 
 def kernel(q, nr, panel, prior, rs, coup, inv, out, part, part1, ra, rb, tv, xv, wv, w0, pbuf, buf0, buf1, rsv,
@@ -14,6 +15,8 @@
     zn = nr
     nx = nr // 2
     r, pr = part.shape[2:]
+    subs = range(SUBS)
+    sub = [pl.ds(h * (r // SUBS), r // SUBS) for h in subs]
     col = lax.axis_index("col")
     i = lax.axis_index("row")
     z, y = lax.div(col, q), lax.rem(col, q)
@@ -95,11 +98,13 @@
         s = (p[:pr] + p[pr:]).T
         return s[:r] + s[r:]
 
-    def a_copy(ph, m, k):
-        return remote(part.at[yfwd(m), zfwd(k)], ra.at[ph, m, k], a_s.at[ph, m, k], a_r.at[ph, m, k], dev(z, yfwd(m), i))
-
-    def b_copy(ph, k):
-        return remote(part.at[y, zfwd(k)], rb.at[ph, k], b_s.at[ph, k], b_r.at[ph, k], dev(zfwd(k), y, i))
+    def a_copy(ph, m, k, h):
+        return remote(part.at[yfwd(m), zfwd(k), sub[h]], ra.at[ph, m, k, sub[h]], a_s.at[ph, m, k, h],
+                      a_r.at[ph, m, k, h], dev(z, yfwd(m), i))
+
+    def b_copy(ph, k, h):
+        return remote(part.at[y, zfwd(k), sub[h]], rb.at[ph, k, sub[h]], b_s.at[ph, k, h], b_r.at[ph, k, h],
+                      dev(zfwd(k), y, i))
 
     def guard(tri, cond, f):
         if tri:
@@ -107,7 +112,15 @@
         else:
             f()
 
-    def reduce(ph, src, buf, sem, w, tri, rhs, add=False, after=None, middle=None):
+    def reduce(ph, src, buf, sem, w, tri, rhs, emit, add=False, after=None):
+        def absorb(k, h):
+            val = part[y, zfwd(k), sub[h]]
+            for m in range(q - 1):
+                a_copy(ph, m, k, h).wait_recv()
+                val = val + ra[ph, m, k, sub[h]]
+            part[y, zfwd(k), sub[h]] = val
+            pl.when(k < zn - 1)(lambda: b_copy(ph, k, h).start())
+
         def compute():
             for m in range(q):
                 @pl.loop(0, zn)
@@ -117,109 +130,110 @@
                     if add:
                         val = val + part1[yfwd(m), zfwd(k)]
                     part[yfwd(m), zfwd(k)] = val
-                    if m < q - 1:
-                        a_copy(ph, m, k).start()
                     if after is not None:
                         load(after, buf, sem, m, k).start()
+                    if m < q - 1:
+                        a_copy(ph, m, k, 0).start()
+                    else:
+                        absorb(k, 0)
+
+                if m < q - 1:
+                    for h in subs[1:]:
+                        pl.loop(0, zn)(lambda k, m=m, h=h: a_copy(ph, m, k, h).start())
+            for h in subs[1:]:
+                pl.loop(0, zn)(lambda k, h=h: absorb(k, h))
 
         guard(tri, below, compute)
-        if middle is not None:
-            middle()
-
-        def collect():
-            def one(k):
-                val = part[y, zfwd(k)]
-                for m in range(q - 1):
-                    a_copy(ph, m, k).wait_recv()
-                    val = val + ra[ph, m, k]
-                part[y, zfwd(k)] = val
-
-            @pl.loop(0, zn - 1)
-            def _(k):
-                one(k)
-                b_copy(ph, k).start()
-
-            one(zn - 1)
-
-        guard(tri, below, collect)
         if tri:
             @pl.when(jnp.logical_not(below))
             def _():
                 part[y, z] = jnp.zeros((r, pr), F32)
-        for k in range(zn - 1):
-            def take(k=k):
-                b_copy(ph, k).wait_recv()
-                part[y, z] = part[y, z] + rb[ph, k]
-
-            guard(tri, zback(k) <= i, take)
-        tv[ph] = part[y, z] if rhs is None else rsv[rhs] - part[y, z]
+        for h in subs:
+            for k in range(zn - 1):
+                def take(k=k):
+                    b_copy(ph, k, h).wait_recv()
+                    part[y, z, sub[h]] = part[y, z, sub[h]] + rb[ph, k, sub[h]]
+
+                guard(tri, zback(k) <= i, take)
+            val = part[y, z, sub[h]]
+            tv[ph, sub[h]] = val if rhs is None else rsv[rhs, sub[h]] - val
+            emit(ph, h)
 
     def drain(ph, tri):
         def waits():
-            for m in range(q - 1):
-                pl.loop(0, zn)(lambda k, m=m: a_copy(ph, m, k).wait_send())
-            pl.loop(0, zn - 1)(lambda k: b_copy(ph, k).wait_send())
+            for h in subs:
+                for m in range(q - 1):
+                    pl.loop(0, zn)(lambda k, m=m: a_copy(ph, m, k, h).wait_send())
+                pl.loop(0, zn - 1)(lambda k: b_copy(ph, k, h).wait_send())
 
         guard(tri, below, waits)
 
-    def spread(ph):
-        def up(n):
-            return remote(tv.at[ph], xv.at[ph, z], c1_s.at[ph, n], x_r.at[ph, z], dev(i, y, lax.rem(i + 2 * n, nr)))
-
-        def fwd(s):
-            return remote(xv.at[ph, s], xv.at[ph, s], c2_s.at[ph, s], x_r.at[ph, s], dev(z, y, sibling))
-
+    def up(ph, n, h):
+        return remote(tv.at[ph, sub[h]], xv.at[ph, z, sub[h]], c1_s.at[ph, n, h], x_r.at[ph, z, h],
+                      dev(i, y, lax.rem(i + 2 * n, nr)))
+
+    def fwd(ph, s, h):
+        there = xv.at[ph, s, sub[h]]
+        return remote(there, there, c2_s.at[ph, s, h], x_r.at[ph, s, h], dev(z, y, sibling))
+
+    def rise(ph, h):
         @pl.when(hub)
         def _():
-            xv[ph, z] = tv[ph]
+            xv[ph, z, sub[h]] = tv[ph, sub[h]]
 
         for n in range(1, nx):
-            up(n).start()
-        pl.when(jnp.logical_not(hub))(lambda: up(0).start())
-
-        @pl.loop(0, zn)
-        def _(k):
-            s = lax.rem(z + k, zn)
-            pl.when(jnp.logical_not(jnp.logical_and(hub, s == z)))(lambda: fwd(s).wait_recv())
-            pl.when(direct)(lambda: fwd(s).start())
-            wv[pl.ds(pl.multiple_of(s * pr, pr), pr), :] = split(xv[ph, s])
-
-        def finish():
+            up(ph, n, h).start()
+        pl.when(jnp.logical_not(hub))(lambda: up(ph, 0, h).start())
+
+    def spread(ph):
+        for h in subs:
+            @pl.loop(0, zn)
+            def _(k):
+                s = lax.rem(z + k, zn)
+                pl.when(jnp.logical_not(jnp.logical_and(hub, s == z)))(lambda: fwd(ph, s, h).wait_recv())
+                pl.when(direct)(lambda: fwd(ph, s, h).start())
+                if h == SUBS - 1:
+                    wv[pl.ds(pl.multiple_of(s * pr, pr), pr), :] = split(xv[ph, s])
+
+    def spread_end(ph):
+        for h in subs:
             for n in range(1, nx):
-                up(n).wait_send()
-            pl.when(jnp.logical_not(hub))(lambda: up(0).wait_send())
-            pl.when(direct)(lambda: pl.loop(0, zn)(lambda s: fwd(s).wait_send()))
-
-        return finish
-
-    def dz_copy(b, ph, k):
-        return remote(tv.at[ph], piece(out, b, y, z), d_s.at[b, k], d_r.at[b, k], dev(zfwd(k), y, i))
-
-    def dy_copy(b, m, slot, s):
-        return remote(piece(out, b, y, s), piece(out, b, y, s), dy_s.at[b, m, slot], dy_r.at[b, m, slot], dev(z, yfwd(m), i))
-
-    def publish_z(b, ph):
-        piece(out, b, y, z)[...] = tv[ph]
+                up(ph, n, h).wait_send()
+            pl.when(jnp.logical_not(hub))(lambda: up(ph, 0, h).wait_send())
+            pl.when(direct)(lambda: pl.loop(0, zn)(lambda s: fwd(ph, s, h).wait_send()))
+
+    def at_out(b, yy, zz, h):
+        return piece(out, b, yy, zz).at[sub[h]]
+
+    def dz_copy(b, ph, k, h, zz):
+        return remote(tv.at[ph, sub[h]], at_out(b, y, zz, h), d_s.at[b, k, h], d_r.at[b, k, h], dev(zfwd(k), y, i))
+
+    def dy_copy(b, m, slot, s, h, yy):
+        return remote(at_out(b, y, s, h), at_out(b, yy, s, h), dy_s.at[b, m, slot, h], dy_r.at[b, m, slot, h],
+                      dev(z, yfwd(m), i))
+
+    def publish_z(b, ph, h):
+        at_out(b, y, z, h)[...] = tv[ph, sub[h]]
         for k in range(zn - 1):
-            dz_copy(b, ph, k).start()
-
-    def publish_y(b, ph):
+            dz_copy(b, ph, k, h, z).start()
         for m in range(q - 1):
-            dy_copy(b, m, 0, z).start()
+            dy_copy(b, m, 0, z, h, y).start()
+
+    def publish_y(b, ph, h):
         for k in range(zn - 1):
-            remote(tv.at[ph], piece(out, b, y, zback(k)), d_s.at[b, k], d_r.at[b, k], dev(zfwd(k), y, i)).wait_recv()
+            dz_copy(b, ph, k, h, zback(k)).wait_recv()
             for m in range(q - 1):
-                dy_copy(b, m, k + 1, zback(k)).start()
+                dy_copy(b, m, k + 1, zback(k), h, y).start()
 
     def publish_end(b, ph):
-        for slot in range(zn):
-            s = z if slot == 0 else zback(slot - 1)
-            for m in range(q - 1):
-                there = piece(out, b, yback(m), s)
-                remote(there, there, dy_s.at[b, m, slot], dy_r.at[b, m, slot], dev(z, yfwd(m), i)).wait_recv()
-                dy_copy(b, m, slot, s).wait_send()
-        for k in range(zn - 1):
-            dz_copy(b, ph, k).wait_send()
+        for h in subs:
+            for slot in range(zn):
+                s = z if slot == 0 else zback(slot - 1)
+                for m in range(q - 1):
+                    dy_copy(b, m, slot, s, h, yback(m)).wait_recv()
+                    dy_copy(b, m, slot, s, h, y).wait_send()
+            for k in range(zn - 1):
+                dz_copy(b, ph, k, h, z).wait_send()
 
     def second_carried():
         for m in range(q):
@@ -228,25 +242,27 @@
                 load(panel.at[1], pbuf, psem, m, k).wait()
                 part1[yfwd(m), zfwd(k)] = product(pbuf, w0, m, k)
 
-    reduce(0, panel.at[0], pbuf, psem, w0, False, 0, after=panel.at[1], middle=second_carried)
+    reduce(0, panel.at[0], pbuf, psem, w0, False, 0, rise, after=panel.at[1])
+    second_carried()
     load_all(coup, buf1, sem1)
-    end0 = spread(0)
+    spread(0)
     drain(0, False)
-    reduce(1, inv.at[0], buf0, sem0, wv, True, None, after=inv.at[1])
-    end1 = spread(1)
+    reduce(1, inv.at[0], buf0, sem0, wv, True, None, rise, after=inv.at[1])
+    spread(1)
     drain(1, True)
-    publish_z(0, 1)
-    reduce(2, coup, buf1, sem1, wv, False, 1, add=True)
-    end2 = spread(2)
+    for h in subs:
+        publish_z(0, 1, h)
+    reduce(2, coup, buf1, sem1, wv, False, 1, rise, add=True)
+    for h in subs:
+        publish_y(0, 1, h)
+    spread(2)
     drain(2, False)
-    publish_y(0, 1)
-    reduce(3, inv.at[1], buf0, sem0, wv, True, None)
-    publish_z(1, 3)
-    publish_y(1, 3)
+    reduce(3, inv.at[1], buf0, sem0, wv, True, None, lambda ph, h: publish_z(1, ph, h))
+    for h in subs:
+        publish_y(1, 3, h)
     drain(3, True)
-    end0()
-    end1()
-    end2()
+    for ph in range(3):
+        spread_end(ph)
     publish_end(0, 1)
     publish_end(1, 3)
 
@@ -283,11 +299,11 @@
             pltpu.VMEM((rows, width), F32),
             pltpu.VMEM((2, r, pr), F32),
             dma((nc,)), dma((nc,)), dma((nc,)), dma((2,)),
-            dma((4, q - 1, nr)), dma((4, q - 1, nr)),
-            dma((4, nr - 1)), dma((4, nr - 1)),
-            dma((3, nr // 2)), dma((3, nr)), dma((3, nr)),
-            dma((2, nr - 1)), dma((2, nr - 1)),
-            dma((2, q - 1, nr)), dma((2, q - 1, nr)),
+            dma((4, q - 1, nr, SUBS)), dma((4, q - 1, nr, SUBS)),
+            dma((4, nr - 1, SUBS)), dma((4, nr - 1, SUBS)),
+            dma((3, nr // 2, SUBS)), dma((3, nr, SUBS)), dma((3, nr, SUBS)),
+            dma((2, nr - 1, SUBS)), dma((2, nr - 1, SUBS)),
+            dma((2, q - 1, nr, SUBS)), dma((2, q - 1, nr, SUBS)),
         ],
         compiler_params=pltpu.CompilerParams(collective_id=0, has_side_effects=True, vmem_limit_bytes=67043328),
     )(panel, prior.T, side, coupling, inverses)

time: 131 us -> 112 us (0.85)
  Pallas kernels: 128 us -> 110 us
    pallas_call x1, Pallas kernels: 128 us -> 110 us  [shards(): pl.pallas_call(functools.partial(kernel, q, nr), out_shape=jax.ShapeDtype...]
where the time goes in v3:
time: 112 us
  Pallas kernels  110 us (98%)
  local copies, waits for them, and re-layouts  2.7 us (2%)
    pallas_call x1, Pallas kernels, shards(): pl.pallas_call(functools.partial(kernel, q, nr), out_shape=jax.ShapeDtype...  110 us
    unnamed x1, local copies, waits for them, and re-layouts  2.7 us

profile of v3, /device:TPU:18, one launch (start us, length us, event | category | flops | bytes accessed | tf_op | source)
XLA Modules:
  0.0 112.3 jit_solution(11309508733822204274)
XLA Ops:
  0.0 109.5 %shard_map.55 = f32[2,64,3072]{2,1,0:T(8,128)} custom-call(f32[2,3072,768]{2,1,0:T(8,128)} %panel.1, f32[64,768]{1,0:T(8,128)} %bitcast.5, f32[2,64,3072]{2,1,0:T(8,128)} %bitcast.4, f32[3072,1536]{1,0:T(8,128)} %coup.1, f32[2,3072,1536]{2,1,0:T(8,128)} %inv.1), custom_call_target="tpu_custom_call" | custom-call | tf_op jit(solution)/shard_map/pallas_call | solution.py:283
  109.6 2.7 %copy.7 = f32[2,3072,64]{1,2,0:T(8,128)} copy(f32[2,3072,64]{1,2,0:T(8,128)} %bitcast.3) | data formatting | bytes 3145728

commit v4 on v3

--- a/solution.py
+++ b/solution.py
@@ -216,6 +216,8 @@
         at_out(b, y, z, h)[...] = tv[ph, sub[h]]
         for k in range(zn - 1):
             dz_copy(b, ph, k, h, z).start()
+
+    def publish_own(b, h):
         for m in range(q - 1):
             dy_copy(b, m, 0, z, h, y).start()
 
@@ -242,6 +244,10 @@
                 load(panel.at[1], pbuf, psem, m, k).wait()
                 part1[yfwd(m), zfwd(k)] = product(pbuf, w0, m, k)
 
+    def last(ph, h):
+        publish_z(1, ph, h)
+        publish_own(1, h)
+
     reduce(0, panel.at[0], pbuf, psem, w0, False, 0, rise, after=panel.at[1])
     second_carried()
     load_all(coup, buf1, sem1)
@@ -250,14 +256,18 @@
     reduce(1, inv.at[0], buf0, sem0, wv, True, None, rise, after=inv.at[1])
     spread(1)
     drain(1, True)
-    for h in subs:
-        publish_z(0, 1, h)
+    publish_z(0, 1, 0)
     reduce(2, coup, buf1, sem1, wv, False, 1, rise, add=True)
-    for h in subs:
-        publish_y(0, 1, h)
+    publish_own(0, 0)
+    publish_y(0, 1, 0)
     spread(2)
     drain(2, False)
-    reduce(3, inv.at[1], buf0, sem0, wv, True, None, lambda ph, h: publish_z(1, ph, h))
+    for h in subs[1:]:
+        publish_z(0, 1, h)
+        publish_own(0, h)
+    reduce(3, inv.at[1], buf0, sem0, wv, True, None, last)
+    for h in subs[1:]:
+        publish_y(0, 1, h)
     for h in subs:
         publish_y(1, 3, h)
     drain(3, True)

time: 112 us -> 110 us (0.982); the launches traced: 112 us -> 108 us
  Pallas kernels: 110 us -> 105 us
    pallas_call x1, Pallas kernels: 110 us -> 105 us  [shards(): pl.pallas_call(functools.partial(kernel, q, nr), out_shape=jax.ShapeDtype...]
where the time goes in v4:
time: 110 us; the launch traced here: 108 us
  Pallas kernels  105 us (95%)
  local copies, waits for them, and re-layouts  2.7 us (2%)
    pallas_call x1, Pallas kernels, shards(): pl.pallas_call(functools.partial(kernel, q, nr), out_shape=jax.ShapeDtype...  105 us
    unnamed x1, local copies, waits for them, and re-layouts  2.7 us

profile of v4, /device:TPU:18, one launch (start us, length us, event | category | flops | bytes accessed | tf_op | source)
XLA Modules:
  0.0 107.8 jit_solution(12729744542369874046)
XLA Ops:
  0.0 105.1 %shard_map.55 = f32[2,64,3072]{2,1,0:T(8,128)} custom-call(f32[2,3072,768]{2,1,0:T(8,128)} %panel.1, f32[64,768]{1,0:T(8,128)} %bitcast.5, f32[2,64,3072]{2,1,0:T(8,128)} %bitcast.4, f32[3072,1536]{1,0:T(8,128)} %coup.1, f32[2,3072,1536]{2,1,0:T(8,128)} %inv.1), custom_call_target="tpu_custom_call" | custom-call | tf_op jit(solution)/shard_map/pallas_call | solution.py:293
  105.1 2.7 %copy.7 = f32[2,3072,64]{1,2,0:T(8,128)} copy(f32[2,3072,64]{1,2,0:T(8,128)} %bitcast.3) | data formatting | bytes 3145728
